TPU v7x, 256 devices: a whole 4x4x8 slice. The times are simulated.
256 devices in a mesh: cal: 2 (over x_lo), gr: 16 (over x_hi, y, core), gc: 8 (over z).
Axes of the slice: x: 4 (x_hi: 2, x_lo: 2; x = x_hi * 2 + x_lo), y: 4, z: 8, core: 2. Of those that a mesh axis runs over, the one named last changes fastest.
Arguments:
- tokens: bfloat16 [512, 8192], P(('gr', 'gc'), 'cal'), may hold values from -12 to 12
- gate_weight: bfloat16 [8192, 28672], P(None, ('cal', 'gr', 'gc')), may hold values from -0.0625 to 0.0625
- up_weight: bfloat16 [8192, 28672], P(None, ('cal', 'gr', 'gc')), may hold values from -0.0625 to 0.0625
- hessian_slab: float32 [28672, 8192], P(('cal', 'gr'), 'gc'), may hold values from -1.2 to 1.2
- weight_error: float32 [512, 28672], P(None, ('cal', 'gr')), may hold values from -0.18 to 0.18
- slab_offset: int32 [1], replicated, may hold values from 0 to 20480
- token_count: int32 [1], replicated, may hold values from 512 to 1023
Outputs:
- new_slab: float32 [28672, 8192], P(('cal', 'gr'), 'gc')
- gradient: float32 [512, 8192], P(('cal', 'gr'), 'gc')
Inputs may be any that keep to these rules, and one draw needn't show every extreme that they name: The slab holds the Hessian's columns slab_offset[0] to slab_offset[0] + 8191.
All inputs are finite; a program needn't handle non-finite values.
Results may differ from a plain program's by a relative error of at most 0.0038.
Values may be sent and summed in bfloat16 or wider, within the bound.
No kernel may reach another device: no remote copies, remote signals or barrier semaphores. Data moves between devices by JAX's collectives and lax.ppermute only.
A program may use at most 64 MiB of HBM per device.

v0:
```python
import jax
import jax.numpy as jnp
from jax import lax
from jax.sharding import Mesh
from jax.sharding import PartitionSpec as P

GR_GC = ("gr_0", "gr_1", "gr_2", "gc")
GR = ("gr_0", "gr_1", "gr_2")
CAL_GR = ("cal", "gr_0", "gr_1", "gr_2")
CAL_GR_GC = ("cal", "gr_0", "gr_1", "gr_2", "gc")


def in_blocks(array, dim, devices):
    dims = array.shape
    tiles = array.reshape(*dims[:dim], devices, dims[dim] // devices, *dims[dim + 1 :])
    return jnp.moveaxis(tiles, dim, 0)


def summed_on_arrival(array, axis, dim):
    tiles = in_blocks(array, dim, lax.axis_size(axis))
    arrived = lax.all_to_all(tiles, axis, split_axis=0, concat_axis=0, tiled=True)
    return arrived.sum(axis=0)


def sent_together(arrays, axis, dim, along):
    widths = [a.shape[along] for a in arrays]
    both = jnp.concatenate(arrays, axis=along)
    filled = summed_on_arrival(both, axis, dim)
    return tuple(jnp.split(filled, [sum(widths[:k]) for k in range(1, len(widths))], axis=along))


def joined_along(tiles, dim):
    dims = list(tiles.shape[1:])
    dims[dim] *= tiles.shape[0]
    return jnp.moveaxis(tiles, 0, dim).reshape(dims)


def copy_for_each(array, axis):
    copies = jnp.broadcast_to(array, (lax.axis_size(axis), *array.shape))
    return lax.all_to_all(copies, axis, split_axis=0, concat_axis=0, tiled=True)


def gathered_copies(array, axis, dim):
    return joined_along(copy_for_each(array, axis), dim)


def sum_at_owner(array, axis, dim):
    devices = lax.axis_size(axis)
    tiles = lax.all_to_all(in_blocks(array, dim, devices), axis, 0, 0, tiled=True)
    return jnp.sum(tiles.astype(jnp.float32), axis=0)


def sum_by_axis(array, axes, dim):
    far, near = axes
    own = sum_at_owner(in_blocks(array, dim, lax.axis_size(far)), near, dim + 1)
    return jnp.sum(
        lax.all_to_all(own.astype(jnp.bfloat16), far, 0, 0, tiled=True).astype(jnp.float32), axis=0
    )


def rows_for(lines, devices):
    spare = -len(lines) % devices
    return jnp.pad(lines, [(0, spare)] + [(0, 0)] * (lines.ndim - 1))


def gather_axes(array, axes, dim):
    far, near = axes
    tiles = copy_for_each(copy_for_each(array, far), near)
    return joined_along(tiles.swapaxes(0, 1).reshape(-1, *array.shape), dim)


def total_of(array, axes):
    lines = array.reshape(-1, array.shape[-1])
    own = sum_by_axis(rows_for(lines, lax.axis_size(axes[0]) * lax.axis_size(axes[1])), axes, 0)
    whole = gather_axes(own.astype(jnp.bfloat16), axes, 0)
    return whole[: len(lines)].reshape(array.shape).astype(jnp.float32)


def on_device(tokens, gate_weight, up_weight, hessian_slab, weight_error, slab_offset, token_count):
    token_rows = lax.all_gather(tokens, GR_GC, axis=0, tiled=True)
    sent_gate, sent_up = (
        lax.all_to_all(gate_weight, "cal", split_axis=0, concat_axis=1, tiled=True),
        lax.all_to_all(up_weight, "cal", split_axis=0, concat_axis=1, tiled=True),
    )
    part_gate = jnp.dot(token_rows, sent_gate, preferred_element_type=jnp.float32)
    part_up = jnp.dot(token_rows, sent_up, preferred_element_type=jnp.float32)
    gate_pre, up_pre = sent_together((part_gate, part_up), "cal", 1, 0)
    hidden = (jax.nn.silu(gate_pre) * up_pre).astype(jnp.bfloat16)
    row_panel = gathered_copies(hidden, "gc", 1)
    panel_width = row_panel.shape[1]
    block_width = hessian_slab.shape[1]
    panel_index = lax.axis_index("cal") * lax.axis_size(GR) + lax.axis_index(GR)
    first_col = slab_offset[0] + lax.axis_index("gc") * block_width
    padded = jnp.pad(row_panel, ((0, 0), (block_width, block_width)))
    shifted = jnp.clip(
        first_col - panel_index * panel_width + block_width, 0, panel_width + block_width
    )
    own_share = lax.dynamic_slice_in_dim(padded, shifted, block_width, 1)
    window = total_of(own_share, (("cal", "gr_0", "gr_1"), "gr_2")).astype(jnp.bfloat16)
    gram_block = lax.dot_general(
        row_panel, window, (((0,), (0,)), ((), ())), preferred_element_type=jnp.float32
    )
    new_slab = hessian_slab + gram_block / token_count[0].astype(jnp.float32)
    gradient = summed_on_arrival(
        jnp.dot(
            weight_error,
            new_slab,
            precision=lax.Precision.HIGHEST,
            preferred_element_type=jnp.float32,
        ),
        CAL_GR,
        0,
    )
    return (new_slab, gradient)


def solution(mesh):
    split = Mesh(
        mesh.devices.reshape(mesh.shape["cal"], 2, 4, 2, mesh.shape["gc"]),
        ("cal", "gr_0", "gr_1", "gr_2", "gc"),
    )
    return jax.shard_map(
        on_device,
        mesh=split,
        in_specs=(
            P(GR_GC, "cal"),
            P(None, CAL_GR_GC),
            P(None, CAL_GR_GC),
            P(CAL_GR, "gc"),
            P(None, CAL_GR),
            P(),
            P(),
        ),
        out_specs=(P(CAL_GR, "gc"), P(CAL_GR, "gc")),
        check_vma=False,
    )
```

profile of v0, /device:TPU:1, one launch (start us, length us, event | category | flops | bytes accessed | tf_op | source)
XLA Modules:
  0.0 291.9 jit_solution(8939373543817521909)
XLA Ops:
  7.2 0.0 copy-start
  7.2 0.0 all-gather.3.cloned.1.call-start
  7.2 0.7 all-gather.3.cloned.1.call-update
  7.9 3.0 %copy.27 = bf16[14,2,8,4096]{3,2,0,1:T(8,128)(2,1)} copy(bf16[14,2,8,4096]{3,2,1,0:T(8,128)(2,1)} %bitcast.48) | data formatting | bytes 3670016 | tf_op jit(solution)/shard_map/all_to_all | solution.py:82
  10.9 4.8 %all-to-all-start = ((bf16[2,4096,112]{1,2,0:T(8,128)(2,1)}), bf16[2,4096,112]{1,2,0:T(8,128)(2,1)}, u32[]{:S(2)}, u32[]{:S(2)}) async-start(bf16[2,4096,112]{1,2,0:T(8,128)(2,1)} %bitcast.43), calls=%async_computation | async-start | bytes 3670016 | tf_op jit(solution)/shard_map/all_to_all | solution.py:82
  15.7 2.9 %copy.26 = bf16[14,2,8,4096]{3,2,0,1:T(8,128)(2,1)} copy(bf16[14,2,8,4096]{3,2,1,0:T(8,128)(2,1)} %bitcast.49) | data formatting | bytes 3670016 | tf_op jit(solution)/shard_map/all_to_all | solution.py:83
  18.6 17.3 %all-to-all-done = bf16[2,4096,112]{1,2,0:T(8,128)(2,1)} async-done(((bf16[2,4096,112]{1,2,0:T(8,128)(2,1)}), bf16[2,4096,112]{1,2,0:T(8,128)(2,1)}, u32[]{:S(2)}, u32[]{:S(2)}) %all-to-all-start) | async-done | bytes 1835040 | tf_op jit(solution)/shard_map/all_to_all | solution.py:82
  35.9 4.7 %all-to-all-start.1 = ((bf16[2,4096,112]{1,2,0:T(8,128)(2,1)}), bf16[2,4096,112]{1,2,0:T(8,128)(2,1)}, u32[]{:S(2)}, u32[]{:S(2)}) async-start(bf16[2,4096,112]{1,2,0:T(8,128)(2,1)} %bitcast.42), calls=%async_computation.1 | async-start | bytes 3670016 | tf_op jit(solution)/shard_map/all_to_all | solution.py:83
  40.6 95.0 %all-gather.3.cloned.1.call-done = bf16[128,4,4096]{2,1,0:T(4,128)(2,1)} async-done(((bf16[1,4,4096]{2,1,0:T(4,128)(2,1)}), bf16[128,4,4096]{2,1,0:T(4,128)(2,1)}) %all-gather.3.cloned.1.call-update) | async-done | bytes 4194320 | tf_op jit(solution)/shard_map/all_gather | solution.py:80
  135.7 6.9 %reshape.24 = bf16[512,4096]{1,0:T(8,128)(2,1)} reshape(bf16[128,4,4096]{2,1,0:T(4,128)(2,1)} %all-gather.3.cloned.1.call-done) | data formatting | bytes 8388608
  142.6 4.2 %fusion.1 = f32[512,224]{0,1:T(8,128)S(1)} fusion(bf16[512,4096]{1,0:T(8,128)(2,1)} %reshape.24, bf16[4096,224]{0,1:T(8,128)(2,1)} %bitcast.2), kind=kOutput, calls=%fused_computation.7 | convolution fusion | flops 939524096 | bytes 6488064 | tf_op jit(solution)/shard_map/dot_general | solution.py:85
  146.8 0.0 all-to-all-done.1
  146.8 4.2 %fusion.2 = f32[512,224]{0,1:T(8,128)S(1)} fusion(bf16[512,4096]{1,0:T(8,128)(2,1)} %reshape.24, bf16[4096,224]{0,1:T(8,128)(2,1)} %bitcast.4), kind=kOutput, calls=%fused_computation.8 | convolution fusion | flops 939524096 | bytes 6488064 | tf_op jit(solution)/shard_map/dot_general | solution.py:86
  151.0 0.1 pad_maximum_fusion
  151.1 14.4 %all_to_all.73 = f32[2,1024,112]{1,2,0:T(8,128)S(1)} all-to-all(f32[2,1024,112]{1,2,0:T(8,128)S(1)} %bitcast.47), channel_id=1, replica_groups=mesh['cal'=2,'gr_0'=2,'gr_1'=4,'gr_2'=2,'gc'=8] {'cal'}, dimensions={0} | all-to-all | bytes 1835008 | tf_op jit(solution)/shard_map/all_to_all | solution.py:21
  165.5 0.1 reduce_sum.42
  165.6 0.1 fusion
  165.7 1.0 broadcast_in_dim.9
  166.7 4.1 %all-to-all-start.3 = ((bf16[8,512,112]{1,2,0:T(8,128)(2,1)}), bf16[8,512,112]{1,2,0:T(8,128)(2,1)S(1)}, u32[]{:S(2)}, u32[]{:S(2)}) async-start(bf16[8,512,112]{1,2,0:T(8,128)(2,1)} %broadcast_in_dim.9), calls=%async_computation.3 | async-start | bytes 1835008 | tf_op jit(solution)/shard_map/all_to_all | solution.py:40
  171.4 25.7 %all-to-all-done.3 = bf16[8,512,112]{1,2,0:T(8,128)(2,1)S(1)} async-done(((bf16[8,512,112]{1,2,0:T(8,128)(2,1)}), bf16[8,512,112]{1,2,0:T(8,128)(2,1)S(1)}, u32[]{:S(2)}, u32[]{:S(2)}) %all-to-all-start.3) | async-done | bytes 917536 | tf_op jit(solution)/shard_map/all_to_all | solution.py:40
  197.2 0.0 copy-start.1
  197.2 0.9 copy-done.1
  198.1 0.5 pad_dynamic-slice_fusion
  198.6 1.3 copy.19
  199.9 1.3 copy.20
  201.2 4.7 %all_to_all.74 = bf16[2,16,16,1024]{3,2,1,0:T(8,128)(2,1)S(1)} all-to-all(bf16[2,16,16,1024]{3,2,1,0:T(8,128)(2,1)S(1)} %copy.20), channel_id=1, replica_groups=mesh['cal'=2,'gr_0'=2,'gr_1'=4,'gr_2'=2,'gc'=8] {'gr_2'}, dimensions={0} | all-to-all | bytes 2097152 | tf_op jit(solution)/shard_map/all_to_all | solution.py:49
  205.9 0.3 reduce_sum.43
  206.2 14.7 %all_to_all.75 = bf16[16,16,1024]{2,1,0:T(8,128)(2,1)S(1)} all-to-all(bf16[16,16,1024]{2,1,0:T(8,128)(2,1)S(1)} %reduce_sum.43), channel_id=1, replica_groups=mesh['cal'=2,'gr_0'=2,'gr_1'=4,'gr_2'=2,'gc'=8] {'cal','gr_0','gr_1'}, dimensions={0} | all-to-all | bytes 1048576 | tf_op jit(solution)/shard_map/all_to_all | solution.py:57
  220.9 0.1 reduce_sum.44
  221.0 0.9 broadcast_in_dim.10
  221.9 3.6 %all-to-all-start.6 = ((bf16[16,16,1024]{2,1,0:T(8,128)(2,1)}), bf16[16,16,1024]{2,1,0:T(8,128)(2,1)S(1)}, u32[]{:S(2)}, u32[]{:S(2)}) async-start(bf16[16,16,1024]{2,1,0:T(8,128)(2,1)} %broadcast_in_dim.10), calls=%async_computation.6 | async-start | bytes 1048576 | tf_op jit(solution)/shard_map/all_to_all | solution.py:40
  225.4 0.0 copy-start.2
  226.2 8.3 %all-to-all-done.6 = bf16[16,16,1024]{2,1,0:T(8,128)(2,1)S(1)} async-done(((bf16[16,16,1024]{2,1,0:T(8,128)(2,1)}), bf16[16,16,1024]{2,1,0:T(8,128)(2,1)S(1)}, u32[]{:S(2)}, u32[]{:S(2)}) %all-to-all-start.6) | async-done | bytes 524320 | tf_op jit(solution)/shard_map/all_to_all | solution.py:40
  234.4 0.0 copy-start.4
  234.4 0.1 broadcast_in_dim.11
  234.6 7.8 %all_to_all.76 = bf16[2,16,16,1024]{3,2,1,0:T(8,128)(2,1)S(1)} all-to-all(bf16[2,16,16,1024]{3,2,1,0:T(8,128)(2,1)S(1)} %broadcast_in_dim.11), channel_id=1, replica_groups=mesh['cal'=2,'gr_0'=2,'gr_1'=4,'gr_2'=2,'gc'=8] {'gr_2'}, dimensions={0} | all-to-all | bytes 2097152 | tf_op jit(solution)/shard_map/all_to_all | solution.py:40
  242.4 0.1 copy.21
  242.5 0.0 copy-done.2
  242.5 0.0 copy-done.4
  242.5 1.1 divide_add_fusion
  243.6 0.0 copy-done
  243.6 0.0 copy-start.3
  243.6 6.8 %fusion.3 = f32[1024,512]{0,1:T(8,128)S(1)} fusion(f32[896,1024]{1,0:T(8,128)S(1)} %divide_add_fusion, f32[512,896]{1,0:T(8,128)S(1)} %copy-done), kind=kOutput, calls=%fused_computation.9 | convolution fusion | flops 5637144576 | bytes 7602176 | tf_op jit(solution)/shard_map/dot_general | solution.py:105
  250.4 0.0 copy-done.3
  250.5 32.3 %all_to_all.77 = f32[32,16,1024]{2,1,0:T(8,128)} all-to-all(f32[32,16,1024]{2,1,0:T(8,128)S(1)} %bitcast.41), channel_id=1, replica_groups=mesh['cal'=2,'gr_0'=2,'gr_1'=4,'gr_2'=2,'gc'=8] {'cal','gr_0','gr_1','gr..., dimensions={0} | all-to-all | bytes 4194304 | tf_op jit(solution)/shard_map/all_to_all | solution.py:21
  282.8 2.3 reduce_sum.45
Async XLA Ops:
  7.2 236.4 %copy-start = (f32[512,896]{1,0:T(8,128)S(1)}, f32[512,896]{1,0:T(8,128)}, u32[]{:S(2)}) copy-start(f32[512,896]{1,0:T(8,128)} %param.11) | copy-start | bytes 5505028
  7.2 128.5 %all-gather.3.cloned.1.call-start = ((), (), s32[]{:S(2)}) async-start(), calls=%async_computation.9 | async-start | bytes 4227072 | tf_op jit(solution)/shard_map/all_gather | solution.py:80
  10.9 25.0 %all-to-all-start = ((bf16[2,4096,112]{1,2,0:T(8,128)(2,1)}), bf16[2,4096,112]{1,2,0:T(8,128)(2,1)}, u32[]{:S(2)}, u32[]{:S(2)}) async-start(bf16[2,4096,112]{1,2,0:T(8,128)(2,1)} %bitcast.43), calls=%async_computation | async-start | bytes 3670016 | tf_op jit(solution)/shard_map/all_to_all | solution.py:82
  35.9 110.9 %all-to-all-start.1 = ((bf16[2,4096,112]{1,2,0:T(8,128)(2,1)}), bf16[2,4096,112]{1,2,0:T(8,128)(2,1)}, u32[]{:S(2)}, u32[]{:S(2)}) async-start(bf16[2,4096,112]{1,2,0:T(8,128)(2,1)} %bitcast.42), calls=%async_computation.1 | async-start | bytes 3670016 | tf_op jit(solution)/shard_map/all_to_all | solution.py:83
  166.7 30.5 %all-to-all-start.3 = ((bf16[8,512,112]{1,2,0:T(8,128)(2,1)}), bf16[8,512,112]{1,2,0:T(8,128)(2,1)S(1)}, u32[]{:S(2)}, u32[]{:S(2)}) async-start(bf16[8,512,112]{1,2,0:T(8,128)(2,1)} %broadcast_in_dim.9), calls=%async_computation.3 | async-start | bytes 1835008 | tf_op jit(solution)/shard_map/all_to_all | solution.py:40
  197.2 0.9 copy-start.1
  221.9 12.6 %all-to-all-start.6 = ((bf16[16,16,1024]{2,1,0:T(8,128)(2,1)}), bf16[16,16,1024]{2,1,0:T(8,128)(2,1)S(1)}, u32[]{:S(2)}, u32[]{:S(2)}) async-start(bf16[16,16,1024]{2,1,0:T(8,128)(2,1)} %broadcast_in_dim.10), calls=%async_computation.6 | async-start | bytes 1048576 | tf_op jit(solution)/shard_map/all_to_all | solution.py:40
  225.4 17.0 %copy-start.2 = (bf16[8,512,112]{1,2,0:T(8,128)(2,1)S(1)}, bf16[8,512,112]{1,2,0:T(8,128)(2,1)}, u32[]{:S(2)}) copy-start(bf16[8,512,112]{1,2,0:T(8,128)(2,1)} %copy-done.1) | copy-start | bytes 2752516
  234.4 8.0 %copy-start.4 = (f32[896,1024]{1,0:T(8,128)S(1)}, f32[896,1024]{1,0:T(8,128)}, u32[]{:S(2)}) copy-start(f32[896,1024]{1,0:T(8,128)} %param.10) | copy-start | bytes 11010052
  243.6 6.8 %copy-start.3 = (f32[896,1024]{1,0:T(8,128)}, f32[896,1024]{1,0:T(8,128)S(1)}, u32[]{:S(2)}) copy-start(f32[896,1024]{1,0:T(8,128)S(1)} %divide_add_fusion) | copy-start | bytes 11010052
Sparse Core Ops, SparseCore 0:
  11.7 123.9 all-gather.2
where the time goes:
time: 293 us; the launch traced here: 292 us
  waiting for transfers between devices  147 us (50%)
  blocking collectives  74 us (25%)
  local copies, waits for them, and re-layouts  18.9 us (6%)
  starting transfers between devices  17.2 us (6%)
  matrix products  16.3 us (6%)
  between operations  15.6 us (5%)
    all_gather x1, waiting for transfers between devices, on_device(): token_rows = lax.all_gather(tokens, GR_GC, axis=0, tiled=True)  95 us
    all_to_all x2, blocking collectives, summed_on_arrival(): lax.all_to_all(tiles, axis, split_axis=0, concat_axis=0, tiled=True)  46.7 us
    all_to_all x2, waiting for transfers between devices, copy_for_each(): return lax.all_to_all(copies, axis, split_axis=0, concat_axis=0, tiled=True)  34 us
    all_to_all x1, waiting for transfers between devices, on_device(): lax.all_to_all(gate_weight, 'cal', split_axis=0, concat_axis=1, tiled=True)  17.3 us
    all_to_all x1, blocking collectives, sum_by_axis(): lax.all_to_all(own.astype(jnp.bfloat16), far, 0, 0, tiled=True)  14.7 us
    unnamed x11, local copies, waits for them, and re-layouts  7.88 us
    all_to_all x1, blocking collectives, copy_for_each(): return lax.all_to_all(copies, axis, split_axis=0, concat_axis=0, tiled=True)  7.81 us
    all_to_all x2, starting transfers between devices, copy_for_each(): return lax.all_to_all(copies, axis, split_axis=0, concat_axis=0, tiled=True)  7.67 us
  transfers between devices with their start and end apart: 5, of which 4 were waited for; matrix products, arithmetic and copies ran while one was open for 6% of the time, Pallas kernels for 0%

commit v1 on v0

--- a/solution.py
+++ b/solution.py
@@ -77,7 +77,10 @@
 
 
 def on_device(tokens, gate_weight, up_weight, hessian_slab, weight_error, slab_offset, token_count):
-    token_rows = lax.all_gather(tokens, GR_GC, axis=0, tiled=True)
+    size = lax.axis_size(GR_GC)
+    blocks = jnp.stack([tokens for _ in range(size)])
+    blocks = lax.all_to_all(blocks, GR_GC, split_axis=0, concat_axis=0)
+    token_rows = jnp.concatenate(blocks, axis=0)
     sent_gate, sent_up = (
         lax.all_to_all(gate_weight, "cal", split_axis=0, concat_axis=1, tiled=True),
         lax.all_to_all(up_weight, "cal", split_axis=0, concat_axis=1, tiled=True),

time: 293 us -> 312 us (1.065)
  starting transfers between devices: 17.2 us -> 42.9 us
  blocking collectives: 74 us -> 92.2 us
  waiting for transfers between devices: 147 us -> 133 us
  between operations: 15.6 us -> 2.2 us
    all_gather x1 -> x0, waiting for transfers between devices: 95 us -> none  [on_device(): token_rows = lax.all_gather(tokens, GR_GC, axis=0, tiled=True)]
    all_to_all x1, waiting for transfers between devices: 17.3 us -> 92.1 us  [on_device(): blocks = lax.all_to_all(blocks, GR_GC, split_axis=0, concat_axis=0)]
    all_to_all x0 -> x1, blocking collectives: none -> 23.4 us  [on_device(): lax.all_to_all(gate_weight, 'cal', split_axis=0, concat_axis=1, tiled=True)]
    all_to_all x1, starting transfers between devices: 4.76 us -> 19.2 us  [on_device(): blocks = lax.all_to_all(blocks, GR_GC, split_axis=0, concat_axis=0)]
    all_to_all x2, starting transfers between devices: 7.67 us -> 19 us  [copy_for_each(): return lax.all_to_all(copies, axis, split_axis=0, concat_axis=0, tiled=True)]
    reshape x0 -> x1, local copies, waits for them, and re-layouts: none -> 6.95 us  [on_device(): token_rows = jnp.concatenate(blocks, axis=0)]
    unnamed x11 -> x12, local copies, waits for them, and re-layouts: 7.88 us -> 0.94 us
    all_to_all x1, waiting for transfers between devices: 0.01 us -> 6.51 us  [on_device(): lax.all_to_all(up_weight, 'cal', split_axis=0, concat_axis=1, tiled=True)]
  transfers between devices with their start and end apart: 5 -> 4, of which waited for: 4 -> 4; matrix products, arithmetic and copies ran while one was open for 6% -> 5% of each run, Pallas kernels for 0% -> 0%
where the time goes in v1:
time: 312 us; the launch traced here: 311 us
  waiting for transfers between devices  133 us (43%)
  blocking collectives  92.2 us (30%)
  starting transfers between devices  42.9 us (14%)
  local copies, waits for them, and re-layouts  21.8 us (7%)
  matrix products  16.3 us (5%)
    all_to_all x1, waiting for transfers between devices, on_device(): blocks = lax.all_to_all(blocks, GR_GC, split_axis=0, concat_axis=0)  92.1 us
    all_to_all x2, blocking collectives, summed_on_arrival(): lax.all_to_all(tiles, axis, split_axis=0, concat_axis=0, tiled=True)  42.3 us
    all_to_all x2, waiting for transfers between devices, copy_for_each(): return lax.all_to_all(copies, axis, split_axis=0, concat_axis=0, tiled=True)  34 us
    all_to_all x1, blocking collectives, on_device(): lax.all_to_all(gate_weight, 'cal', split_axis=0, concat_axis=1, tiled=True)  23.4 us
    all_to_all x1, starting transfers between devices, on_device(): blocks = lax.all_to_all(blocks, GR_GC, split_axis=0, concat_axis=0)  19.2 us
    all_to_all x2, starting transfers between devices, copy_for_each(): return lax.all_to_all(copies, axis, split_axis=0, concat_axis=0, tiled=True)  19 us
    all_to_all x1, blocking collectives, sum_by_axis(): lax.all_to_all(own.astype(jnp.bfloat16), far, 0, 0, tiled=True)  14.1 us
    all_to_all x1, blocking collectives, copy_for_each(): return lax.all_to_all(copies, axis, split_axis=0, concat_axis=0, tiled=True)  7.81 us
  transfers between devices with their start and end apart: 4, of which 4 were waited for; matrix products, arithmetic and copies ran while one was open for 5% of the time, Pallas kernels for 0%

profile of v1, /device:TPU:1, one launch (start us, length us, event | category | flops | bytes accessed | tf_op | source)
XLA Modules:
  0.0 310.9 jit_solution(12507016339780444356)
XLA Ops:
  0.6 0.0 copy-start
  0.6 0.0 copy-start.4
  0.7 1.8 copy.27
  2.4 23.4 %all_to_all.78 = bf16[2,4096,112]{1,2,0:T(8,128)(2,1)} all-to-all(bf16[2,4096,112]{1,2,0:T(8,128)(2,1)S(1)} %bitcast.42), channel_id=1, replica_groups=mesh['cal'=2,'gr_0'=2,'gr_1'=4,'gr_2'=2,'gc'=8] {'cal'}, dimensions={0} | all-to-all | bytes 3670016 | tf_op jit(solution)/shard_map/all_to_all | solution.py:85
  25.8 0.0 copy-done.4
  25.8 4.1 %stack.2 = bf16[128,4,4096]{2,1,0:T(4,128)(2,1)} broadcast(bf16[4,4096]{1,0:T(4,128)(2,1)S(1)} %copy-done.4), dimensions={1,2} | broadcast | bytes 4227072 | tf_op jit(solution)/shard_map/stack | solution.py:81
  29.8 19.2 %all-to-all-start = ((bf16[128,4,4096]{2,1,0:T(4,128)(2,1)}), bf16[128,4,4096]{2,1,0:T(4,128)(2,1)}, u32[]{:S(2)}, u32[]{:S(2)}) async-start(bf16[128,4,4096]{2,1,0:T(4,128)(2,1)} %stack.2), calls=%async_computation | async-start | bytes 8388608 | tf_op jit(solution)/shard_map/all_to_all | solution.py:82
  49.0 2.9 copy.26
  52.0 92.1 %all-to-all-done = bf16[128,4,4096]{2,1,0:T(4,128)(2,1)} async-done(((bf16[128,4,4096]{2,1,0:T(4,128)(2,1)}), bf16[128,4,4096]{2,1,0:T(4,128)(2,1)}, u32[]{:S(2)}, u32[]{:S(2)}) %all-to-all-start) | async-done | bytes 4194336 | tf_op jit(solution)/shard_map/all_to_all | solution.py:82
  144.1 4.7 %all-to-all-start.2 = ((bf16[2,4096,112]{1,2,0:T(8,128)(2,1)}), bf16[2,4096,112]{1,2,0:T(8,128)(2,1)}, u32[]{:S(2)}, u32[]{:S(2)}) async-start(bf16[2,4096,112]{1,2,0:T(8,128)(2,1)} %bitcast.41), calls=%async_computation.2 | async-start | bytes 3670016 | tf_op jit(solution)/shard_map/all_to_all | solution.py:86
  148.8 6.9 %reshape.25 = bf16[512,4096]{1,0:T(8,128)(2,1)} reshape(bf16[128,4,4096]{2,1,0:T(4,128)(2,1)} %all-to-all-done) | data formatting | bytes 8388608 | tf_op jit(solution)/shard_map/reshape | solution.py:83
  155.7 4.2 %fusion.1 = f32[512,224]{0,1:T(8,128)S(1)} fusion(bf16[512,4096]{1,0:T(8,128)(2,1)} %reshape.25, bf16[4096,224]{0,1:T(8,128)(2,1)} %bitcast.49), kind=kOutput, calls=%fused_computation.7 | convolution fusion | flops 939524096 | bytes 6488064 | tf_op jit(solution)/shard_map/dot_general | solution.py:88
  159.9 6.5 %all-to-all-done.2 = bf16[2,4096,112]{1,2,0:T(8,128)(2,1)} async-done(((bf16[2,4096,112]{1,2,0:T(8,128)(2,1)}), bf16[2,4096,112]{1,2,0:T(8,128)(2,1)}, u32[]{:S(2)}, u32[]{:S(2)}) %all-to-all-start.2) | async-done | bytes 1835040 | tf_op jit(solution)/shard_map/all_to_all | solution.py:86
  166.5 4.2 %fusion.2 = f32[512,224]{0,1:T(8,128)S(1)} fusion(bf16[512,4096]{1,0:T(8,128)(2,1)} %reshape.25, bf16[4096,224]{0,1:T(8,128)(2,1)} %bitcast.3), kind=kOutput, calls=%fused_computation.8 | convolution fusion | flops 939524096 | bytes 6488064 | tf_op jit(solution)/shard_map/dot_general | solution.py:89
  170.7 0.1 pad_maximum_fusion
  170.7 10.0 %all_to_all.79 = f32[2,1024,112]{1,2,0:T(8,128)S(1)} all-to-all(f32[2,1024,112]{1,2,0:T(8,128)S(1)} %bitcast.46), channel_id=1, replica_groups=mesh['cal'=2,'gr_0'=2,'gr_1'=4,'gr_2'=2,'gc'=8] {'cal'}, dimensions={0} | all-to-all | bytes 1835008 | tf_op jit(solution)/shard_map/all_to_all | solution.py:21
  180.7 0.1 reduce_sum.42
  180.8 0.1 fusion
  180.9 1.0 broadcast_in_dim.9
  181.9 15.4 %all-to-all-start.4 = ((bf16[8,512,112]{1,2,0:T(8,128)(2,1)}), bf16[8,512,112]{1,2,0:T(8,128)(2,1)S(1)}, u32[]{:S(2)}, u32[]{:S(2)}) async-start(bf16[8,512,112]{1,2,0:T(8,128)(2,1)} %broadcast_in_dim.9), calls=%async_computation.4 | async-start | bytes 1835008 | tf_op jit(solution)/shard_map/all_to_all | solution.py:40
  198.0 25.7 %all-to-all-done.4 = bf16[8,512,112]{1,2,0:T(8,128)(2,1)S(1)} async-done(((bf16[8,512,112]{1,2,0:T(8,128)(2,1)}), bf16[8,512,112]{1,2,0:T(8,128)(2,1)S(1)}, u32[]{:S(2)}, u32[]{:S(2)}) %all-to-all-start.4) | async-done | bytes 917536 | tf_op jit(solution)/shard_map/all_to_all | solution.py:40
  223.7 0.0 copy-start.1
  223.7 0.9 copy-done.1
  224.6 0.5 pad_dynamic-slice_fusion
  225.1 1.3 copy.19
  226.4 1.3 copy.20
  227.7 4.7 %all_to_all.80 = bf16[2,16,16,1024]{3,2,1,0:T(8,128)(2,1)S(1)} all-to-all(bf16[2,16,16,1024]{3,2,1,0:T(8,128)(2,1)S(1)} %copy.20), channel_id=1, replica_groups=mesh['cal'=2,'gr_0'=2,'gr_1'=4,'gr_2'=2,'gc'=8] {'gr_2'}, dimensions={0} | all-to-all | bytes 2097152 | tf_op jit(solution)/shard_map/all_to_all | solution.py:49
  232.4 0.3 reduce_sum.43
  232.7 14.1 %all_to_all.81 = bf16[16,16,1024]{2,1,0:T(8,128)(2,1)S(1)} all-to-all(bf16[16,16,1024]{2,1,0:T(8,128)(2,1)S(1)} %reduce_sum.43), channel_id=1, replica_groups=mesh['cal'=2,'gr_0'=2,'gr_1'=4,'gr_2'=2,'gc'=8] {'cal','gr_0','gr_1'}, dimensions={0} | all-to-all | bytes 1048576 | tf_op jit(solution)/shard_map/all_to_all | solution.py:57
  246.8 0.1 reduce_sum.44
  246.8 0.9 broadcast_in_dim.10
  247.7 3.6 %all-to-all-start.7 = ((bf16[16,16,1024]{2,1,0:T(8,128)(2,1)}), bf16[16,16,1024]{2,1,0:T(8,128)(2,1)S(1)}, u32[]{:S(2)}, u32[]{:S(2)}) async-start(bf16[16,16,1024]{2,1,0:T(8,128)(2,1)} %broadcast_in_dim.10), calls=%async_computation.7 | async-start | bytes 1048576 | tf_op jit(solution)/shard_map/all_to_all | solution.py:40
  251.3 0.0 copy-start.2
  252.0 8.3 %all-to-all-done.7 = bf16[16,16,1024]{2,1,0:T(8,128)(2,1)S(1)} async-done(((bf16[16,16,1024]{2,1,0:T(8,128)(2,1)}), bf16[16,16,1024]{2,1,0:T(8,128)(2,1)S(1)}, u32[]{:S(2)}, u32[]{:S(2)}) %all-to-all-start.7) | async-done | bytes 524320 | tf_op jit(solution)/shard_map/all_to_all | solution.py:40
  260.3 0.0 copy-start.5
  260.3 0.1 broadcast_in_dim.11
  260.4 7.8 %all_to_all.82 = bf16[2,16,16,1024]{3,2,1,0:T(8,128)(2,1)S(1)} all-to-all(bf16[2,16,16,1024]{3,2,1,0:T(8,128)(2,1)S(1)} %broadcast_in_dim.11), channel_id=1, replica_groups=mesh['cal'=2,'gr_0'=2,'gr_1'=4,'gr_2'=2,'gc'=8] {'gr_2'}, dimensions={0} | all-to-all | bytes 2097152 | tf_op jit(solution)/shard_map/all_to_all | solution.py:40
  268.2 0.1 copy.21
  268.3 0.0 copy-done.2
  268.3 0.0 copy-done.5
  268.3 1.1 divide_add_fusion
  269.5 0.0 copy-done
  269.5 0.0 copy-start.3
  269.5 6.8 %fusion.3 = f32[1024,512]{0,1:T(8,128)S(1)} fusion(f32[896,1024]{1,0:T(8,128)S(1)} %divide_add_fusion, f32[512,896]{1,0:T(8,128)S(1)} %copy-done), kind=kOutput, calls=%fused_computation.9 | convolution fusion | flops 5637144576 | bytes 7602176 | tf_op jit(solution)/shard_map/dot_general | solution.py:108
  276.3 0.0 copy-done.3
  276.3 32.3 %all_to_all.83 = f32[32,16,1024]{2,1,0:T(8,128)} all-to-all(f32[32,16,1024]{2,1,0:T(8,128)S(1)} %bitcast.40), channel_id=1, replica_groups=mesh['cal'=2,'gr_0'=2,'gr_1'=4,'gr_2'=2,'gc'=8] {'cal','gr_0','gr_1','gr..., dimensions={0} | all-to-all | bytes 4194304 | tf_op jit(solution)/shard_map/all_to_all | solution.py:21
  308.6 2.3 reduce_sum.45
Async XLA Ops:
  0.6 268.8 %copy-start = (f32[512,896]{1,0:T(8,128)S(1)}, f32[512,896]{1,0:T(8,128)}, u32[]{:S(2)}) copy-start(f32[512,896]{1,0:T(8,128)} %param.11) | copy-start | bytes 5505028
  0.6 25.1 %copy-start.4 = (bf16[4,4096]{1,0:T(4,128)(2,1)S(1)}, bf16[4,4096]{1,0:T(4,128)(2,1)}, u32[]{:S(2)}) copy-start(bf16[4,4096]{1,0:T(4,128)(2,1)} %param.7) | copy-start | bytes 98308
  29.8 114.2 %all-to-all-start = ((bf16[128,4,4096]{2,1,0:T(4,128)(2,1)}), bf16[128,4,4096]{2,1,0:T(4,128)(2,1)}, u32[]{:S(2)}, u32[]{:S(2)}) async-start(bf16[128,4,4096]{2,1,0:T(4,128)(2,1)} %stack.2), calls=%async_computation | async-start | bytes 8388608 | tf_op jit(solution)/shard_map/all_to_all | solution.py:82
  144.1 22.4 %all-to-all-start.2 = ((bf16[2,4096,112]{1,2,0:T(8,128)(2,1)}), bf16[2,4096,112]{1,2,0:T(8,128)(2,1)}, u32[]{:S(2)}, u32[]{:S(2)}) async-start(bf16[2,4096,112]{1,2,0:T(8,128)(2,1)} %bitcast.41), calls=%async_computation.2 | async-start | bytes 3670016 | tf_op jit(solution)/shard_map/all_to_all | solution.py:86
  181.9 41.8 %all-to-all-start.4 = ((bf16[8,512,112]{1,2,0:T(8,128)(2,1)}), bf16[8,512,112]{1,2,0:T(8,128)(2,1)S(1)}, u32[]{:S(2)}, u32[]{:S(2)}) async-start(bf16[8,512,112]{1,2,0:T(8,128)(2,1)} %broadcast_in_dim.9), calls=%async_computation.4 | async-start | bytes 1835008 | tf_op jit(solution)/shard_map/all_to_all | solution.py:40
  223.7 0.9 copy-start.1
  247.7 12.6 %all-to-all-start.7 = ((bf16[16,16,1024]{2,1,0:T(8,128)(2,1)}), bf16[16,16,1024]{2,1,0:T(8,128)(2,1)S(1)}, u32[]{:S(2)}, u32[]{:S(2)}) async-start(bf16[16,16,1024]{2,1,0:T(8,128)(2,1)} %broadcast_in_dim.10), calls=%async_computation.7 | async-start | bytes 1048576 | tf_op jit(solution)/shard_map/all_to_all | solution.py:40
  251.3 17.0 %copy-start.2 = (bf16[8,512,112]{1,2,0:T(8,128)(2,1)S(1)}, bf16[8,512,112]{1,2,0:T(8,128)(2,1)}, u32[]{:S(2)}) copy-start(bf16[8,512,112]{1,2,0:T(8,128)(2,1)} %copy-done.1) | copy-start | bytes 2752516
  260.3 8.0 %copy-start.5 = (f32[896,1024]{1,0:T(8,128)S(1)}, f32[896,1024]{1,0:T(8,128)}, u32[]{:S(2)}) copy-start(f32[896,1024]{1,0:T(8,128)} %param.10) | copy-start | bytes 11010052
  269.5 6.8 %copy-start.3 = (f32[896,1024]{1,0:T(8,128)}, f32[896,1024]{1,0:T(8,128)S(1)}, u32[]{:S(2)}) copy-start(f32[896,1024]{1,0:T(8,128)S(1)} %divide_add_fusion) | copy-start | bytes 11010052
